TPU v7x, 128 devices: a whole 4x4x4 slice. The times are simulated.
128 devices in a mesh: grp: 8 (over y_lo, z), tok: 16 (over y_hi, x, core).
Axes of the slice: x: 4, y: 4 (y_hi: 2, y_lo: 2; y = y_hi * 2 + y_lo), z: 4, core: 2. Of those that a mesh axis runs over, the one named last changes fastest.
Arguments:
- hidden: bfloat16 [8, 2048, 4608], P('grp', 'tok'), may hold values from -40 to 40
- input_gain: float32 [4608], replicated, may hold values from 0.25 to 1.75
- w_query: bfloat16 [4608, 4096], P(None, 'tok'), may hold values from -4 to 4
- w_key: bfloat16 [4608, 2048], P(None, 'tok'), may hold values from -4 to 4
- w_value: bfloat16 [4608, 2048], P(None, 'tok'), may hold values from -0.09375 to 0.09375
- w_out: bfloat16 [4096, 4608], P('tok'), may hold values from -0.09375 to 0.09375
- post_gain: float32 [4608], replicated, may hold values from 0.25 to 1.75
- cache_keys: bfloat16 [64, 256, 2048], P('grp', None, 'tok'), may hold values from -6 to 46
- cache_values: bfloat16 [64, 256, 2048], P('grp', None, 'tok'), may hold values from -6 to 6
- page_table: int32 [8, 8], replicated, may hold values from 0 to 63, as said below
- stretch_request: int32 [8, 8], P('grp'), may hold values from 0 to 2, never falling along the last dimension, each value on 1 to 4 neighbouring positions
- recompute_ids: int32 [8, 204], P('grp'), may hold values from 0 to 2047, as said below
- query_counts: int32 [8, 3], P('grp'), may hold values from 1 to 1024, 1844 in all within a row
Outputs:
- output: bfloat16 [8, 2048, 4608], P('grp', 'tok')
Inputs may be any that keep to these rules, and one draw needn't show every extreme that they name: `page_table`: row g lists the pages of group g's 8 stretch slots; page p is held by group p // 8; every page appears once, and the slots of a group take exactly one page from each group. `stretch_request`: each request of a group holds one or more consecutive slots, request numbers never fall along the slots, and one request holds (8 + 1) // 2 slots, none more. `recompute_ids`: each row holds 204 distinct cached tokens of the group (slot times 256 plus the token within the stretch) in rising order. `query_counts`: the counts of a group sum to 1844.
All inputs are finite; a program needn't handle non-finite values.
Results may differ from a plain program's by a relative error of at most 0.01.
Values may be sent and summed in bfloat16 or wider, within the bound.
A program may use at most 128 MiB of HBM per device.

v0:
```python
import math

import jax
import jax.numpy as jnp
from jax import lax
from jax.sharding import PartitionSpec as P

HEAD = 128


EPSILON = 1e-06
CAP_VALUE = 50.0
QUERY_SCALE = 1.0 / 12.0
ROPE_BASE = 10000.0


def rotate(tensor, positions):
    halfway = tensor.shape[-1] // 2
    ladder = jnp.arange(halfway).astype(jnp.float32)
    frequency = jnp.exp(ladder * (-2.0 * math.log(ROPE_BASE) / tensor.shape[-1]))
    angles = positions.astype(jnp.float32)[:, None] * frequency[None, :]
    cosine = jnp.cos(angles)[:, None, :]
    sine_values = jnp.sin(angles)[:, None, :]
    front_part = tensor[..., :halfway]
    back_part = tensor[..., halfway:]
    return jnp.concatenate(
        [
            front_part * cosine - back_part * sine_values,
            back_part * cosine + front_part * sine_values,
        ],
        axis=-1,
    )


def normalize(matrix, gain):
    widened = matrix.astype(jnp.float32)
    return widened * lax.rsqrt(jnp.mean(widened * widened, axis=-1, keepdims=True) + EPSILON) * gain


def request_layout(stretch_owner, counts_row, selected, stretch_len, new_rows):
    slot_total = stretch_owner.shape[0]
    requests = counts_row.shape[0]
    request_ids = jnp.arange(requests, dtype=jnp.int32)
    slot_ids = jnp.arange(slot_total, dtype=jnp.int32)
    belongs = (stretch_owner[:, None] == request_ids[None, :]).astype(jnp.int32)
    first_slot = jnp.sum((stretch_owner[None, :] < request_ids[:, None]).astype(jnp.int32), axis=1)
    stretch_count = jnp.sum(belongs, axis=0)
    offsets = (slot_ids - jnp.sum(belongs * first_slot[None, :], axis=1)) * stretch_len
    inner_ids = jnp.arange(stretch_len, dtype=jnp.int32)
    cache_pos = (offsets[:, None] + inner_ids[None, :]).reshape(-1)
    cache_req = jnp.broadcast_to(stretch_owner[:, None], (slot_total, stretch_len)).reshape(-1)
    cache_ids = jnp.arange(slot_total * stretch_len, dtype=jnp.int32)
    chosen = jnp.sum((selected[:, None] == cache_ids[None, :]).astype(jnp.int32), axis=0)
    cache_live = chosen == 0
    home_slot = ((selected // stretch_len)[:, None] == slot_ids[None, :]).astype(jnp.int32)
    select_req = jnp.sum(home_slot * stretch_owner[None, :], axis=1)
    select_pos = jnp.sum(home_slot * offsets[None, :], axis=1) + selected % stretch_len
    query_total = new_rows - selected.shape[0]
    query_ids = jnp.arange(query_total, dtype=jnp.int32)
    query_start = jnp.cumsum(counts_row) - counts_row
    query_req = jnp.sum((query_ids[:, None] >= query_start[None, 1:]).astype(jnp.int32), axis=1)
    mapping = (query_req[:, None] == request_ids[None, :]).astype(jnp.int32)
    query_pos = (
        jnp.sum(mapping * (stretch_count * stretch_len - query_start)[None, :], axis=1) + query_ids
    )
    row_req = jnp.concatenate([select_req, query_req])
    row_pos = jnp.concatenate([select_pos, query_pos])
    key_req = jnp.concatenate([cache_req, row_req])
    key_pos = jnp.concatenate([cache_pos, row_pos])
    key_live = jnp.concatenate([cache_live, jnp.ones((new_rows,), dtype=bool)])
    return (offsets, row_req, row_pos, key_req, key_pos, key_live)


def attend(queries, all_keys, all_values, row_req, row_pos, key_req, key_pos, key_live):
    scores = jnp.einsum("qcgd,kcd->cgqk", queries, all_keys, preferred_element_type=jnp.float32)
    capped = CAP_VALUE * jnp.tanh(scores * (QUERY_SCALE / CAP_VALUE))
    visible = (
        (key_req[None, :] == row_req[:, None])
        & (key_pos[None, :] <= row_pos[:, None])
        & key_live[None, :]
    ).astype(jnp.float32)
    weights = jnp.exp(capped) * visible[None, None]
    denominator = jnp.sum(weights, axis=-1)
    rounded = weights.astype(jnp.bfloat16)
    weighted = jnp.einsum("cgqk,kcd->qcgd", rounded, all_values, preferred_element_type=jnp.float32)
    result = weighted / jnp.transpose(denominator, (2, 0, 1))[..., None]
    return result.astype(jnp.bfloat16).reshape(queries.shape[0], -1)


def run_attention(query_rot, all_keys, all_values, rows_req, rows_pos, key_req, key_pos, key_live):
    total_rows = query_rot.shape[0]
    block_rows = min(512, total_rows)
    block_total = total_rows // block_rows

    def one_block(bundle):
        return attend(
            bundle[0], all_keys, all_values, bundle[1], bundle[2], key_req, key_pos, key_live
        )

    shaped = query_rot.reshape((block_total, block_rows) + query_rot.shape[1:])
    attended = lax.map(
        one_block,
        (
            shaped,
            rows_req.reshape(block_total, block_rows),
            rows_pos.reshape(block_total, block_rows),
        ),
    )
    return attended.reshape(total_rows, -1)


def on_device(
    hidden,
    input_gain,
    w_query,
    w_key,
    w_value,
    w_out,
    post_gain,
    cache_keys,
    cache_values,
    page_table,
    stretch_request,
    recompute_ids,
    query_counts,
):
    own_rows = hidden[0]
    row_count = own_rows.shape[0]
    tok_total = lax.axis_size("tok")
    new_rows = row_count * tok_total
    stretch_len = cache_keys.shape[1]
    key_heads = w_key.shape[1] // HEAD
    query_heads = w_query.shape[1] // HEAD
    group_size = query_heads // key_heads
    query_cols = w_query.shape[1]
    key_cols = w_key.shape[1]
    normed_own = normalize(own_rows, input_gain).astype(jnp.bfloat16)
    offsets, row_req, row_pos, key_req, key_pos, key_live = request_layout(
        stretch_request[0], query_counts[0], recompute_ids[0], stretch_len, new_rows
    )
    group_index = lax.axis_index("grp")
    my_pages = lax.dynamic_index_in_dim(page_table, group_index, 0, keepdims=False)
    sections = (
        lax.all_gather(cache_keys, "grp", axis=0, tiled=True),
        lax.all_gather(cache_values, "grp", axis=0, tiled=True),
    )
    section_rows = sections[0].shape[0]
    hits = (my_pages[:, None] == jnp.arange(section_rows, dtype=jnp.int32)[None, :]).astype(
        jnp.bfloat16
    )
    picked_keys = jnp.einsum("cp,pkh->ckh", hits, sections[0], preferred_element_type=jnp.float32)
    picked_values = jnp.einsum("cp,pkh->ckh", hits, sections[1], preferred_element_type=jnp.float32)
    page_keys = picked_keys.astype(jnp.bfloat16)
    page_values = picked_values.astype(jnp.bfloat16)
    slot_total = page_keys.shape[0]
    shifts = jnp.broadcast_to(offsets[:, None], (slot_total, stretch_len)).reshape(-1)
    segment = lax.all_gather(normed_own, "tok", axis=0, tiled=True)
    joined = jnp.concatenate(
        [
            jnp.dot(segment, w_query, preferred_element_type=jnp.float32),
            jnp.dot(segment, w_key, preferred_element_type=jnp.float32),
            jnp.dot(segment, w_value, preferred_element_type=jnp.float32),
        ],
        axis=1,
    )
    cached_k = rotate(
        page_keys.astype(jnp.float32).reshape(slot_total * stretch_len, key_heads, HEAD), shifts
    ).astype(jnp.bfloat16)
    cached_v = page_values.reshape(slot_total * stretch_len, key_heads, HEAD)
    query_rot = rotate(joined[:, :query_cols].reshape(new_rows, query_heads, HEAD), row_pos).astype(
        jnp.bfloat16
    )
    query_rot = query_rot.reshape(new_rows, key_heads, group_size, HEAD)
    key_rot = rotate(
        joined[:, query_cols : query_cols + key_cols].reshape(new_rows, key_heads, HEAD), row_pos
    ).astype(jnp.bfloat16)
    value_new = (
        joined[:, query_cols + key_cols :].astype(jnp.bfloat16).reshape(new_rows, key_heads, HEAD)
    )
    all_keys = jnp.concatenate([cached_k, key_rot], axis=0)
    all_values = jnp.concatenate([cached_v, value_new], axis=0)
    attended = run_attention(
        query_rot, all_keys, all_values, row_req, row_pos, key_req, key_pos, key_live
    )
    summed = lax.psum_scatter(
        jnp.dot(attended, w_out, preferred_element_type=jnp.float32).astype(jnp.bfloat16),
        "tok",
        scatter_dimension=0,
        tiled=True,
    ).astype(jnp.float32)
    result = own_rows.astype(jnp.float32) + normalize(summed, post_gain)
    return result.astype(jnp.bfloat16)[None]


def solution(mesh):
    return jax.shard_map(
        on_device,
        mesh=mesh,
        in_specs=(
            P("grp", "tok", None),
            P(),
            P(None, "tok"),
            P(None, "tok"),
            P(None, "tok"),
            P("tok", None),
            P(),
            P("grp", None, "tok"),
            P("grp", None, "tok"),
            P(),
            P("grp", None),
            P("grp", None),
            P("grp", None),
        ),
        out_specs=P("grp", "tok", None),
        check_vma=False,
    )
```

profile of v0, /device:TPU:1, one launch (start us, length us, event | category | flops | bytes accessed | tf_op | source)
XLA Modules:
  0.0 586.5 jit_solution(13476773845455432164)
XLA Ops:
  6.5 2.4 copy.28
  9.0 2.2 copy.32
  11.3 0.3 fusion.28
  11.7 2.1 fusion.30
  13.8 0.2 reduce-window.4
  14.0 0.1 slice.22
  14.1 0.1 convert_reduce_fusion.2
  14.2 0.1 select_reduce_fusion.3
  14.5 0.1 fusion.51
  14.6 0.1 select_reduce_fusion
  14.8 0.1 select_reduce_fusion.1
  14.9 0.1 concatenate.75
  15.1 0.1 concatenate.73
  15.3 0.3 convert_reduce_fusion
  15.6 0.7 dynamic-slice_bitcast_fusion
  16.3 2.8 multiply_cosine_fusion.2
  19.1 51.7 %all-gather.6.cloned.1.call-done = bf16[64,256,128]{2,0,1:T(8,128)(2,1)} async-done(((bf16[8,256,128]{2,0,1:T(8,128)(2,1)}), bf16[64,256,128]{2,0,1:T(8,128)(2,1)}) %all-gather.6.cloned.1.call-update) | async-done | bytes 4194320 | tf_op jit(solution)/shard_map/all_gather | solution.py:144
  70.8 2.9 fusion.33
  73.7 0.2 copy.29
  73.9 1.3 fusion.62
  75.3 2.3 copy.40
  77.6 1.1 copy.41
  78.7 54.7 %all-gather.8.cloned.1.call-done = bf16[64,256,128]{2,0,1:T(8,128)(2,1)} async-done(((bf16[8,256,128]{2,0,1:T(8,128)(2,1)}), bf16[64,256,128]{2,0,1:T(8,128)(2,1)}) %all-gather.8.cloned.1.call-update) | async-done | bytes 4194320 | tf_op jit(solution)/shard_map/all_gather | solution.py:145
  133.5 2.9 convolution_convert_fusion.2
  136.3 0.9 copy.33
  137.2 121.5 %all-gather.4.cloned.1.call-done = bf16[2048,4608]{1,0:T(8,128)(2,1)} async-done(((bf16[128,4608]{1,0:T(8,128)(2,1)}), bf16[2048,4608]{1,0:T(8,128)(2,1)}) %all-gather.4.cloned.1.call-update) | async-done | bytes 18874384 | tf_op jit(solution)/shard_map/all_gather | solution.py:157
  258.7 10.4 %convolution_bitcast_fusion = f32[2048,1,128]{0,2,1:T(8,128)S(1)} fusion(bf16[2048,4608]{1,0:T(8,128)(2,1)} %all-gather.4.cloned.1.call-done, bf16[4608,128]{1,0:T(8,128)(2,1)} %param.18), kind=kOutput, calls=%fused_computation.26 | convolution fusion | flops 2415919104 | bytes 21102592 | tf_op jit(solution)/shard_map/dot_general | solution.py:161
  269.2 5.2 fusion.48
  274.4 1.0 maximum_maximum_fusion
  275.4 1.6 copy.35
  277.1 9.8 %fusion.63 = f32[2048,256]{0,1:T(8,128)S(1)} fusion(bf16[2048,4608]{1,0:T(8,128)(2,1)} %all-gather.4.cloned.1.call-done, bf16[4608,256]{1,0:T(8,128)(2,1)} %param.17), kind=kOutput, calls=%fused_computation.111 | convolution fusion | flops 4831838208 | bytes 23330816 | tf_op jit(solution)/shard_map/dot_general | solution.py:160
  286.9 1.3 subtract_convert_fusion
  288.2 2.2 concatenate.67
  290.4 2.2 concatenate.68
  292.7 2.8 pad_maximum_fusion
  295.5 2.6 copy.34
  298.2 9.4 %fusion.32 = bf16[2048,1,128]{2,0,1:T(8,128)(2,1)S(1)} fusion(bf16[2048,4608]{1,0:T(8,128)(2,1)} %all-gather.4.cloned.1.call-done, bf16[4608,128]{1,0:T(8,128)(2,1)} %param.19), kind=kOutput, calls=%fused_computation.34 | convolution fusion | flops 2416181248 | bytes 20578304 | tf_op jit(solution)/shard_map/dot_general | solution.py:162
  307.6 1.0 pad_maximum_fusion.1
  308.6 2.3 copy.36
  310.9 98.5 %while.10 = (s32[]{:T(128)}, bf16[4,512,256]{2,1,0:T(8,128)(2,1)}, bf16[4,512,1,2,128]{4,1,3,2,0:T(8,128)(2,1)}, bf16[4096,1,128]{2,0,1:T(8,128)(2,1)S(1)}, s32[...) while((s32[]{:T(128)}, bf16[4,512,256]{2,1,0:T(8,128)(2,1)}, ...), condition=%wide.region_12.13_spmd, body=%wide.region_10.12_spmd.sunk | while | flops 2191784960 | bytes 66643084 | solution.py:101
  310.9 1.8 and_convert_fusion.2
  312.7 9.9 %fusion.80 = (f32[2,512]{1,0:T(2,128)S(1)}, f32[512,2,4096]{2,0,1:T(8,128)}) fusion(f32[512,4096]{1,0:T(8,128)S(1)} %and_convert_fusion.2, bf16[4096,1,128]{2,0,1:T(8,128)(2,1)S(1)} %get-tuple-element.226, bf16[4,512,1,2,128]{4,1,3,2,0:T(8,128)(2,1)} %get-tuple-element.225, s32[]{:T(128)} %get-tuple-element.212), kind=kOutput, calls=%fused_computation.1.clone.1 | convolution fusion | flops 1090518016 | bytes 26481152 | tf_op jit(solution)/shard_map/while/body/eval_jaxpr/qcgd,kcd->cgqk/dot_general | solution.py:75
  322.6 9.4 %fusion.81 = bf16[512,1,2,128]{0,3,2,1:T(8,128)(2,1)} fusion(bf16[4096,1,128]{0,2,1:T(8,128)(2,1)S(1)} %copy-done.1, f32[512,2,4096]{2,0,1:T(8,128)} %get-tuple-element.199, f32[512,4096]{1,0:T(8,128)S(1)} %and_convert_fusion.2, f32[512,2]{0,1:T(2,128)S(1)} %bitcast.153), kind=kOutput, calls=%fused_computation.11.clone.1 | convolution fusion | flops 1090781184 | bytes 26480640 | tf_op jit(solution)/shard_map/while/body/eval_jaxpr/cgqk,kcd->qcgd/dot_general | solution.py:85
  332.0 1.8 copy.46
  333.8 1.7 constant_dynamic-update-slice_fusion.2
  335.5 1.8 and_convert_fusion.2
  337.4 9.9 %fusion.80 = (f32[2,512]{1,0:T(2,128)S(1)}, f32[512,2,4096]{2,0,1:T(8,128)}) fusion(f32[512,4096]{1,0:T(8,128)S(1)} %and_convert_fusion.2, bf16[4096,1,128]{2,0,1:T(8,128)(2,1)S(1)} %get-tuple-element.226, bf16[4,512,1,2,128]{4,1,3,2,0:T(8,128)(2,1)} %get-tuple-element.225, s32[]{:T(128)} %get-tuple-element.212), kind=kOutput, calls=%fused_computation.1.clone.1 | convolution fusion | flops 1090518016 | bytes 26481152 | tf_op jit(solution)/shard_map/while/body/eval_jaxpr/qcgd,kcd->cgqk/dot_general | solution.py:75
  347.3 9.4 %fusion.81 = bf16[512,1,2,128]{0,3,2,1:T(8,128)(2,1)} fusion(bf16[4096,1,128]{0,2,1:T(8,128)(2,1)S(1)} %copy-done.1, f32[512,2,4096]{2,0,1:T(8,128)} %get-tuple-element.199, f32[512,4096]{1,0:T(8,128)S(1)} %and_convert_fusion.2, f32[512,2]{0,1:T(2,128)S(1)} %bitcast.153), kind=kOutput, calls=%fused_computation.11.clone.1 | convolution fusion | flops 1090781184 | bytes 26480640 | tf_op jit(solution)/shard_map/while/body/eval_jaxpr/cgqk,kcd->qcgd/dot_general | solution.py:85
  356.6 1.8 copy.46
  358.4 1.7 constant_dynamic-update-slice_fusion.2
  360.1 1.8 and_convert_fusion.2
  362.0 9.9 %fusion.80 = (f32[2,512]{1,0:T(2,128)S(1)}, f32[512,2,4096]{2,0,1:T(8,128)}) fusion(f32[512,4096]{1,0:T(8,128)S(1)} %and_convert_fusion.2, bf16[4096,1,128]{2,0,1:T(8,128)(2,1)S(1)} %get-tuple-element.226, bf16[4,512,1,2,128]{4,1,3,2,0:T(8,128)(2,1)} %get-tuple-element.225, s32[]{:T(128)} %get-tuple-element.212), kind=kOutput, calls=%fused_computation.1.clone.1 | convolution fusion | flops 1090518016 | bytes 26481152 | tf_op jit(solution)/shard_map/while/body/eval_jaxpr/qcgd,kcd->cgqk/dot_general | solution.py:75
  371.9 9.4 %fusion.81 = bf16[512,1,2,128]{0,3,2,1:T(8,128)(2,1)} fusion(bf16[4096,1,128]{0,2,1:T(8,128)(2,1)S(1)} %copy-done.1, f32[512,2,4096]{2,0,1:T(8,128)} %get-tuple-element.199, f32[512,4096]{1,0:T(8,128)S(1)} %and_convert_fusion.2, f32[512,2]{0,1:T(2,128)S(1)} %bitcast.153), kind=kOutput, calls=%fused_computation.11.clone.1 | convolution fusion | flops 1090781184 | bytes 26480640 | tf_op jit(solution)/shard_map/while/body/eval_jaxpr/cgqk,kcd->qcgd/dot_general | solution.py:85
  381.3 1.8 copy.46
  383.1 1.7 constant_dynamic-update-slice_fusion.2
  384.8 1.8 and_convert_fusion.2
  386.6 9.9 %fusion.80 = (f32[2,512]{1,0:T(2,128)S(1)}, f32[512,2,4096]{2,0,1:T(8,128)}) fusion(f32[512,4096]{1,0:T(8,128)S(1)} %and_convert_fusion.2, bf16[4096,1,128]{2,0,1:T(8,128)(2,1)S(1)} %get-tuple-element.226, bf16[4,512,1,2,128]{4,1,3,2,0:T(8,128)(2,1)} %get-tuple-element.225, s32[]{:T(128)} %get-tuple-element.212), kind=kOutput, calls=%fused_computation.1.clone.1 | convolution fusion | flops 1090518016 | bytes 26481152 | tf_op jit(solution)/shard_map/while/body/eval_jaxpr/qcgd,kcd->cgqk/dot_general | solution.py:75
  396.5 9.4 %fusion.81 = bf16[512,1,2,128]{0,3,2,1:T(8,128)(2,1)} fusion(bf16[4096,1,128]{0,2,1:T(8,128)(2,1)S(1)} %copy-done.1, f32[512,2,4096]{2,0,1:T(8,128)} %get-tuple-element.199, f32[512,4096]{1,0:T(8,128)S(1)} %and_convert_fusion.2, f32[512,2]{0,1:T(2,128)S(1)} %bitcast.153), kind=kOutput, calls=%fused_computation.11.clone.1 | convolution fusion | flops 1090781184 | bytes 26480640 | tf_op jit(solution)/shard_map/while/body/eval_jaxpr/cgqk,kcd->qcgd/dot_general | solution.py:85
  405.9 1.8 copy.46
  407.7 1.7 constant_dynamic-update-slice_fusion.2
  409.4 10.3 %convolution_convert_fusion = bf16[2048,4608]{1,0:T(8,128)(2,1)} fusion(bf16[2048,256]{1,0:T(8,128)(2,1)} %bitcast.152, bf16[256,4608]{1,0:T(8,128)(2,1)S(1)} %copy-done), kind=kOutput, calls=%fused_computation.20 | convolution fusion | flops 4841275392 | bytes 22282240 | tf_op jit(solution)/shard_map/dot_general | solution.py:186
  419.7 156.0 %reduce-scatter.2.cloned.1.call-done = bf16[128,4608]{1,0:T(8,128)(2,1)} async-done(((bf16[2048,4608]{1,0:T(8,128)(2,1)}), bf16[128,4608]{1,0:T(8,128)(2,1)}) %reduce-scatter.2.cloned.1.call-update) | async-done | bytes 1179664 | tf_op jit(solution)/shard_map/reduce_scatter | solution.py:185
  575.6 1.6 fusion.26
  577.2 2.8 fusion.34
  (60 shorter events, 0.8 us)
Async XLA Ops:
  6.5 402.8 %copy-start = (bf16[256,4608]{1,0:T(8,128)(2,1)S(1)}, bf16[256,4608]{1,0:T(8,128)(2,1)}, u32[]{:S(2)}) copy-start(bf16[256,4608]{1,0:T(8,128)(2,1)} %param.20) | copy-start | bytes 7077892
  6.5 4.8 copy-start.2
  6.5 64.3 %all-gather.6.cloned.1.call-start = ((), (), s32[]{:S(2)}) async-start(), calls=%async_computation.2 | async-start | bytes 4718592 | tf_op jit(solution)/shard_map/all_gather | solution.py:144
  9.0 124.5 %all-gather.8.cloned.1.call-start = ((), (), s32[]{:S(2)}) async-start(), calls=%async_computation.3 | async-start | bytes 4718592 | tf_op jit(solution)/shard_map/all_gather | solution.py:145
  11.2 2.6 copy-start.9
  11.2 2.9 copy-start.8
  11.3 3.5 copy-start.7
  11.3 247.5 %all-gather.4.cloned.1.call-start = ((), (), s32[]{:S(2)}) async-start(), calls=%async_computation.1 | async-start | bytes 20054016 | tf_op jit(solution)/shard_map/all_gather | solution.py:157
  13.8 561.9 %reduce-scatter.2.cloned.1.call-start = ((), (), s32[]{:S(2)}) async-start(), calls=%async_computation.4 | async-start | bytes 20054016 | tf_op jit(solution)/shard_map/reduce_scatter | solution.py:185
  277.1 9.8 %copy-start.5 = (f32[2048,64]{0,1:T(8,128)S(1)}, f32[2048,64]{0,1:T(8,128)}, u32[]{:S(2)}) copy-start(f32[2048,64]{0,1:T(8,128)} %get-tuple-element.126) | copy-start | bytes 1572868
  277.1 9.8 %copy-start.6 = (f32[2048,64]{0,1:T(8,128)S(1)}, f32[2048,64]{0,1:T(8,128)}, u32[]{:S(2)}) copy-start(f32[2048,64]{0,1:T(8,128)} %get-tuple-element.127) | copy-start | bytes 1572868
  298.2 9.4 %copy-start.4 = (bf16[8,256,128]{2,1,0:T(8,128)(2,1)S(1)}, bf16[8,256,128]{2,1,0:T(8,128)(2,1)}, u32[]{:S(2)}) copy-start(bf16[8,256,128]{2,1,0:T(8,128)(2,1)} %copy.33) | copy-start | bytes 1572868
  312.7 9.9 %copy-start.1 = (bf16[4096,1,128]{0,2,1:T(8,128)(2,1)S(1)}, bf16[4096,1,128]{0,2,1:T(8,128)(2,1)}, u32[]{:S(2)}) copy-start(bf16[4096,1,128]{0,2,1:T(8,128)(2,1)} %get-tuple-element.232) | copy-start | bytes 3145732 | tf_op jit(solution)/shard_map/while
  337.3 9.9 %copy-start.1 = (bf16[4096,1,128]{0,2,1:T(8,128)(2,1)S(1)}, bf16[4096,1,128]{0,2,1:T(8,128)(2,1)}, u32[]{:S(2)}) copy-start(bf16[4096,1,128]{0,2,1:T(8,128)(2,1)} %get-tuple-element.232) | copy-start | bytes 3145732 | tf_op jit(solution)/shard_map/while
  362.0 9.9 %copy-start.1 = (bf16[4096,1,128]{0,2,1:T(8,128)(2,1)S(1)}, bf16[4096,1,128]{0,2,1:T(8,128)(2,1)}, u32[]{:S(2)}) copy-start(bf16[4096,1,128]{0,2,1:T(8,128)(2,1)} %get-tuple-element.232) | copy-start | bytes 3145732 | tf_op jit(solution)/shard_map/while
  386.6 9.9 %copy-start.1 = (bf16[4096,1,128]{0,2,1:T(8,128)(2,1)S(1)}, bf16[4096,1,128]{0,2,1:T(8,128)(2,1)}, u32[]{:S(2)}) copy-start(bf16[4096,1,128]{0,2,1:T(8,128)(2,1)} %get-tuple-element.232) | copy-start | bytes 3145732 | tf_op jit(solution)/shard_map/while
  419.6 157.6 %copy-start.3 = (bf16[1,128,4608]{2,1,0:T(8,128)(2,1)S(1)}, bf16[1,128,4608]{2,1,0:T(8,128)(2,1)}, u32[]{:S(2)}) copy-start(bf16[1,128,4608]{2,1,0:T(8,128)(2,1)} %param.15) | copy-start | bytes 3538948
Sparse Core Ops, SparseCore 0:
  9.1 61.7 all-gather.5
  72.4 61.0 all-gather.7
  135.9 122.8 all-gather.3
  419.8 155.7 reduce-scatter.1
where the time goes:
time: 588 us; the launch traced here: 587 us
  waiting for transfers between devices  384 us (65%)
  matrix products  123 us (21%)
  local copies, waits for them, and re-layouts  36.6 us (6%)
  other arithmetic  29.6 us (5%)
  between operations  13.4 us (2%)
    reduce_scatter x1, waiting for transfers between devices, on_device(): lax.psum_scatter(jnp.dot(attended, w_out, preferred_element_type=jnp.floa...  156 us
    all_gather x1, waiting for transfers between devices, on_device(): segment = lax.all_gather(normed_own, 'tok', axis=0, tiled=True)  122 us
    all_gather x1, waiting for transfers between devices, on_device(): lax.all_gather(cache_values, 'grp', axis=0, tiled=True)  54.7 us
    all_gather x1, waiting for transfers between devices, on_device(): lax.all_gather(cache_keys, 'grp', axis=0, tiled=True)  51.7 us
    dot_general x4, matrix products, attend(): jnp.einsum('qcgd,kcd->cgqk', queries, all_keys, preferred_element_type=jn...  39.7 us
    dot_general x4, matrix products, attend(): jnp.einsum('cgqk,kcd->qcgd', rounded, all_values, preferred_element_type=...  37.4 us
    dynamic_update_slice x8, local copies, waits for them, and re-layouts, run_attention(): lax.map(one_block, (shaped, rows_req.reshape(block_total, block_rows), ro...  13.9 us
  transfers between devices with their start and end apart: 4, of which 4 were waited for; matrix products, arithmetic and copies ran while one was open for 4% of the time, Pallas kernels for 0%

commit v1 on v0

v1 whole, which is shorter than its diff:
```python
import math

import jax
import jax.numpy as jnp
from jax import lax
from jax.experimental import pallas as pl
from jax.experimental.pallas import tpu as pltpu
from jax.sharding import PartitionSpec as P

HEAD = 128
EPSILON = 1e-06
CAP_VALUE = 50.0
QUERY_SCALE = 1.0 / 12.0
ROPE_BASE = 10000.0
SPAN = 1 << 16
FAR = 1 << 30
BLOCK = 256


def angles_of(positions):
    halfway = HEAD // 2
    ladder = jnp.arange(halfway).astype(jnp.float32)
    frequency = jnp.exp(ladder * (-2.0 * math.log(ROPE_BASE) / HEAD))
    angles = positions.astype(jnp.float32)[:, None] * frequency[None, :]
    cosine = jnp.cos(angles)
    sine = jnp.sin(angles)
    return (
        jnp.concatenate([cosine, cosine], axis=1),
        jnp.concatenate([-sine, sine], axis=1),
    )


def turn(tensor, cosine, sine):
    halfway = HEAD // 2
    swapped = jnp.concatenate([tensor[..., halfway:], tensor[..., :halfway]], axis=-1)
    return tensor * cosine + swapped * sine


def normalize(matrix, gain):
    widened = matrix.astype(jnp.float32)
    return widened * lax.rsqrt(jnp.mean(widened * widened, axis=-1, keepdims=True) + EPSILON) * gain


def request_layout(owners, counts_row, selected, table_row, groups, stretch_len, new_rows):
    slots = owners.shape[0]
    requests = counts_row.shape[0]
    request_ids = jnp.arange(requests, dtype=jnp.int32)
    slot_ids = jnp.arange(slots, dtype=jnp.int32)
    belongs = (owners[:, None] == request_ids[None, :]).astype(jnp.int32)
    first_slot = jnp.sum((owners[None, :] < request_ids[:, None]).astype(jnp.int32), axis=1)
    stretch_count = jnp.sum(belongs, axis=0)
    offsets = (slot_ids - jnp.sum(belongs * first_slot[None, :], axis=1)) * stretch_len
    home = ((selected // stretch_len)[:, None] == slot_ids[None, :]).astype(jnp.int32)
    select_req = jnp.sum(home * owners[None, :], axis=1)
    select_pos = jnp.sum(home * offsets[None, :], axis=1) + selected % stretch_len
    query_ids = jnp.arange(new_rows - selected.shape[0], dtype=jnp.int32)
    query_start = jnp.cumsum(counts_row) - counts_row
    query_req = jnp.sum((query_ids[:, None] >= query_start[None, 1:]).astype(jnp.int32), axis=1)
    mapping = (query_req[:, None] == request_ids[None, :]).astype(jnp.int32)
    query_pos = (
        jnp.sum(mapping * (stretch_count * stretch_len - query_start)[None, :], axis=1) + query_ids
    )
    row_req = jnp.concatenate([select_req, query_req])
    row_pos = jnp.concatenate([select_pos, query_pos])
    source = table_row // groups[1]
    place = (source[None, :] == jnp.arange(groups[0], dtype=jnp.int32)[:, None]).astype(jnp.int32)
    slot_of = jnp.sum(place * slot_ids[None, :], axis=1)
    shift_of = jnp.sum(place * offsets[None, :], axis=1)
    owner_of = jnp.sum(place * owners[None, :], axis=1)
    inner = jnp.arange(stretch_len, dtype=jnp.int32)
    cached_id = slot_of[:, None] * stretch_len + inner[None, :]
    cached_code = owner_of[:, None] * SPAN + shift_of[:, None] + inner[None, :]
    dead = jnp.any(cached_id.reshape(-1)[:, None] == selected[None, :], axis=1)
    row_code = row_req * SPAN + row_pos
    key_code = jnp.concatenate([cached_code.reshape(-1), row_code])
    live = jnp.concatenate([~dead, jnp.ones((new_rows,), bool)])
    return shift_of, row_req, row_pos, row_code, key_code, live


def attention_kernel(
    active, q_ref, k_ref, v_ref, pk_ref, pv_ref, pcos_ref, psin_ref, rcode_ref, kcode_ref,
    live_ref, out_ref, keys, values, queries, total,
):
    rows = q_ref.shape[0]
    cached = pk_ref.shape[0]
    blocks = rows // BLOCK
    for s in range(cached // BLOCK):
        part = pl.ds(s * BLOCK, BLOCK)
        page = pk_ref[part, :].astype(jnp.float32)
        turned = page * pcos_ref[s : s + 1, :] + pltpu.roll(page, HEAD // 2, 1) * psin_ref[s : s + 1, :]
        keys[part, :] = turned.astype(jnp.bfloat16)
        alive = live_ref[part, :].astype(jnp.bfloat16)
        values[part, :HEAD] = pv_ref[part, :] * alive
        values[part, HEAD:] = jnp.broadcast_to(alive, (BLOCK, HEAD))
    keys[pl.ds(cached, rows), :] = k_ref[...]
    values[pl.ds(cached, rows), :HEAD] = v_ref[...]
    values[pl.ds(cached, rows), HEAD:] = jnp.ones((rows, HEAD), jnp.bfloat16)

    def row_block(rb, carry):
        here = pl.ds(pl.multiple_of(rb * BLOCK, BLOCK), BLOCK)
        queries[:BLOCK, :] = q_ref[here, :HEAD]
        queries[BLOCK:, :] = q_ref[here, HEAD:]
        total[...] = jnp.zeros_like(total)
        code = rcode_ref[here, :]
        base = (code // SPAN) * SPAN

        def key_block(kb, inner_carry):
            @pl.when(active[rb, kb] > 0)
            def _():
                there = pl.ds(pl.multiple_of(kb * BLOCK, BLOCK), BLOCK)
                scores = lax.dot_general(
                    queries[...], keys[there, :], (((1,), (1,)), ((), ())),
                    preferred_element_type=jnp.float32,
                )
                capped = jnp.tanh(scores * (QUERY_SCALE / CAP_VALUE))
                weights = jnp.exp2(capped * (CAP_VALUE * math.log2(math.e)))
                kcode = kcode_ref[pl.ds(kb, 1), 0, :]
                seen = (kcode <= code) & (kcode >= base)
                both = jnp.concatenate([seen, seen], axis=0)
                rounded = jnp.where(both, weights, 0.0).astype(jnp.bfloat16)
                total[...] += jnp.dot(rounded, values[there, :], preferred_element_type=jnp.float32)

            return inner_carry

        lax.fori_loop(0, kcode_ref.shape[0], key_block, 0)
        result = total[:, :HEAD] / total[:, HEAD:]
        out_ref[here, :HEAD] = result[:BLOCK].astype(jnp.bfloat16)
        out_ref[here, HEAD:] = result[BLOCK:].astype(jnp.bfloat16)
        return carry

    lax.fori_loop(0, blocks, row_block, 0)


def attention(q, k, v, page_k, page_v, pcos, psin, row_code, key_code, live):
    rows = q.shape[0]
    total_keys = key_code.shape[0]
    key_blocks = key_code.reshape(-1, BLOCK)
    row_blocks = row_code.reshape(-1, BLOCK)
    low = jnp.min(key_blocks, axis=1)
    high = jnp.max(key_blocks, axis=1)
    row_high = jnp.max(row_blocks, axis=1)
    row_low = (jnp.min(row_blocks, axis=1) // SPAN) * SPAN
    active = ((low[None, :] <= row_high[:, None]) & (high[None, :] >= row_low[:, None])).astype(
        jnp.int32
    )
    vmem = pl.BlockSpec(memory_space=pltpu.VMEM)
    return pl.pallas_call(
        attention_kernel,
        out_shape=jax.ShapeDtypeStruct((rows, q.shape[1]), jnp.bfloat16),
        in_specs=[pl.BlockSpec(memory_space=pltpu.SMEM)] + [vmem] * 10,
        out_specs=vmem,
        scratch_shapes=[
            pltpu.VMEM((total_keys, HEAD), jnp.bfloat16),
            pltpu.VMEM((total_keys, 2 * HEAD), jnp.bfloat16),
            pltpu.VMEM((2 * BLOCK, HEAD), jnp.bfloat16),
            pltpu.VMEM((2 * BLOCK, 2 * HEAD), jnp.float32),
        ],
        compiler_params=pltpu.CompilerParams(vmem_limit_bytes=40 << 20),
        name="attention",
    )(
        active, q, k, v, page_k, page_v, pcos, psin, row_code[:, None],
        jnp.where(live, key_code, FAR).reshape(-1, 1, BLOCK), live.astype(jnp.float32)[: page_k.shape[0], None],
    )


def on_device(
    hidden, input_gain, w_query, w_key, w_value, w_out, post_gain, cache_keys, cache_values,
    page_table, stretch_request, recompute_ids, query_counts,
):
    own_rows = hidden[0]
    tok_total = lax.axis_size("tok")
    groups = lax.axis_size("grp")
    new_rows = own_rows.shape[0] * tok_total
    pages, stretch_len = cache_keys.shape[:2]
    normed_own = normalize(own_rows, input_gain).astype(jnp.bfloat16)
    segment = lax.all_gather(normed_own, "tok", axis=0, tiled=True)
    group = lax.axis_index("grp")
    mine = page_table // pages == group
    local = jnp.sum(jnp.where(mine, page_table % pages, 0), axis=1)
    picks = (local[:, None] == jnp.arange(pages, dtype=jnp.int32)[None, :]).astype(jnp.bfloat16)
    both = jnp.concatenate([cache_keys, cache_values], axis=-1)
    send = jnp.einsum("gp,pkh->gkh", picks, both, preferred_element_type=jnp.float32).astype(
        jnp.bfloat16
    )
    got = lax.all_to_all(send, "grp", 0, 0, tiled=True)
    got = got.reshape(groups * stretch_len, 2 * HEAD)
    table_row = lax.dynamic_index_in_dim(page_table, group, 0, keepdims=False)
    shift_of, row_req, row_pos, row_code, key_code, live = request_layout(
        stretch_request[0], query_counts[0], recompute_ids[0], table_row, (groups, pages),
        stretch_len, new_rows,
    )
    pcos, psin = angles_of(shift_of)
    cosine, sine = angles_of(row_pos)
    q = jnp.dot(segment, w_query, preferred_element_type=jnp.float32)
    k = jnp.dot(segment, w_key, preferred_element_type=jnp.float32)
    v = jnp.dot(segment, w_value, preferred_element_type=jnp.float32)
    q = turn(q.reshape(new_rows, -1, HEAD), cosine[:, None], sine[:, None])
    q = q.astype(jnp.bfloat16).reshape(new_rows, -1)
    k = turn(k, cosine, sine).astype(jnp.bfloat16)
    attended = attention(
        q, k, v.astype(jnp.bfloat16), got[:, :HEAD], got[:, HEAD:], pcos, psin, row_code, key_code, live
    )
    summed = lax.psum_scatter(
        jnp.dot(attended, w_out, preferred_element_type=jnp.float32).astype(jnp.bfloat16),
        "tok",
        scatter_dimension=0,
        tiled=True,
    ).astype(jnp.float32)
    result = own_rows.astype(jnp.float32) + normalize(summed, post_gain)
    return result.astype(jnp.bfloat16)[None]


def solution(mesh):
    return jax.shard_map(
        on_device,
        mesh=mesh,
        in_specs=(
            P("grp", "tok", None), P(), P(None, "tok"), P(None, "tok"), P(None, "tok"),
            P("tok", None), P(), P("grp", None, "tok"), P("grp", None, "tok"), P(),
            P("grp", None), P("grp", None), P("grp", None),
        ),
        out_specs=P("grp", "tok", None),
        check_vma=False,
    )
```

time: 588 us -> 402 us (0.68)
  waiting for transfers between devices: 384 us -> 262 us
  matrix products: 123 us -> 38.8 us
  Pallas kernels: 0 us -> 33.5 us
  local copies, waits for them, and re-layouts: 36.6 us -> 25.2 us
  other arithmetic: 29.6 us -> 21.2 us
  starting transfers between devices: 0.13 us -> 6.91 us
    all_gather x2 -> x0, waiting for transfers between devices: 106 us -> none  [the longest x1 54.7 us: on_device(): lax.all_gather(cache_values, 'grp', axis=0, tiled=True)]
    dot_general x13 -> x4, matrix products: 112 us -> 29.7 us  [the longest x1 10.7 us: on_device(): q = jnp.dot(segment, w_query, preferred_element_type=jnp.float32)]
    pallas_call x0 -> x1, Pallas kernels: none -> 33.5 us  [attention(): pl.pallas_call(attention_kernel, out_shape=jax.ShapeDtypeStruct((rows, q....]
    all_gather x1, waiting for transfers between devices: 122 us -> 101 us  [on_device(): segment = lax.all_gather(normed_own, 'tok', axis=0, tiled=True)]
    dynamic_update_slice x8 -> x0, local copies, waits for them, and re-layouts: 13.9 us -> none  [run_attention(): lax.map(one_block, (shaped, rows_req.reshape(block_total, block_rows), ro...]
    all_to_all x0 -> x1, waiting for transfers between devices: none -> 7.37 us  [on_device(): got = lax.all_to_all(send, 'grp', 0, 0, tiled=True)]
    all_to_all x0 -> x1, starting transfers between devices: none -> 6.87 us  [on_device(): got = lax.all_to_all(send, 'grp', 0, 0, tiled=True)]
    while x11 -> x0, local copies, waits for them, and re-layouts: 6.53 us -> none  [the longest x3 6.52 us: run_attention(): lax.map(one_block, (shaped, rows_req.reshape(block_total, block_rows), ro...]
  transfers between devices with their start and end apart: 4 -> 3, of which waited for: 4 -> 3; matrix products, arithmetic and copies ran while one was open for 4% -> 4% of each run, Pallas kernels for 0% -> 0%
where the time goes in v1:
time: 402 us; the launch traced here: 401 us
  waiting for transfers between devices  262 us (65%)
  matrix products  38.8 us (10%)
  Pallas kernels  33.5 us (8%)
  local copies, waits for them, and re-layouts  25.2 us (6%)
  other arithmetic  21.2 us (5%)
  between operations  13.8 us (3%)
  starting transfers between devices  6.91 us (2%)
    reduce_scatter x1, waiting for transfers between devices, on_device(): lax.psum_scatter(jnp.dot(attended, w_out, preferred_element_type=jnp.floa...  154 us
    all_gather x1, waiting for transfers between devices, on_device(): segment = lax.all_gather(normed_own, 'tok', axis=0, tiled=True)  101 us
    pallas_call x1, Pallas kernels, attention(): pl.pallas_call(attention_kernel, out_shape=jax.ShapeDtypeStruct((rows, q....  33.5 us
    unnamed x42, local copies, waits for them, and re-layouts  12.7 us
    dot_general x1, matrix products, on_device(): q = jnp.dot(segment, w_query, preferred_element_type=jnp.float32)  10.7 us
    dot_general x1, matrix products, on_device(): k = jnp.dot(segment, w_key, preferred_element_type=jnp.float32)  9.3 us
    dot_general x1, matrix products, on_device(): v = jnp.dot(segment, w_value, preferred_element_type=jnp.float32)  9.22 us
    dot_general x1, matrix products, on_device(): jnp.dot(attended, w_out, preferred_element_type=jnp.float32)  9.09 us
  transfers between devices with their start and end apart: 3, of which 3 were waited for; matrix products, arithmetic and copies ran while one was open for 4% of the time, Pallas kernels for 0%

profile of v1, /device:TPU:1, one launch (start us, length us, event | category | flops | bytes accessed | tf_op | source)
XLA Modules:
  0.0 401.3 jit_solution(16483152413470195442)
XLA Ops:
  6.5 1.7 fusion.2
  8.3 0.0 copy-start.12
  8.3 2.7 fusion.4
  11.0 0.0 all-gather.2.cloned.1.call-update
  11.0 0.3 copy.69
  11.4 0.3 copy.70
  11.7 0.1 fusion.22
  11.9 0.5 convolution_convert_fusion.2
  12.4 0.0 copy-start.16
  12.4 0.0 copy-start.14
  12.4 0.0 copy-start.13
  12.4 1.2 copy.71
  13.6 6.9 %all-to-all-start = ((bf16[8,256,256]{2,1,0:T(8,128)(2,1)}), bf16[8,256,256]{2,1,0:T(8,128)(2,1)}, u32[]{:S(2)}, u32[]{:S(2)}) async-start(bf16[8,256,256]{2,1,0:T(8,128)(2,1)} %copy.71), calls=%async_computation | async-start | bytes 2097152 | tf_op jit(solution)/shard_map/all_to_all | solution.py:185
  20.5 0.0 reduce-scatter.2.cloned.1.call-start
  20.5 0.2 reduce-window.4
  20.7 0.1 slice.23
  20.8 0.1 fusion.14
  20.9 0.1 convert_reduce_fusion.1
  21.0 0.1 select_reduce_fusion.6
  21.2 0.1 select_reduce_fusion
  21.3 0.1 select_reduce_fusion.1
  21.4 0.1 fusion.19
  21.5 0.1 select_reduce_fusion.3
  21.7 0.1 add_bitcast_fusion
  21.8 0.1 fusion.30
  21.9 0.1 pad_maximum_fusion.2.pcos_ref
  22.0 0.2 fusion.36
  22.1 0.3 compare_reduce_fusion
  22.5 0.1 fusion.18
  22.6 0.1 fusion.27
  22.6 0.1 pad_maximum_fusion.3.psin_ref
  22.7 0.4 copy.73.live_ref
  23.1 1.5 copy.72.rcode_ref
  24.5 0.1 fusion.16
  24.7 0.1 and_convert_fusion.active
  24.7 5.9 %fusion.13 = (f32[2048,64]{1,0:T(8,128)}, f32[2048,64]{1,0:T(8,128)}, f32[2048,64]{1,0:T(8,128)}) fusion(f32[64]{0:T(128)S(1)} %multiply_exponential_fusion, f32[2048]{0:T(1024)S(1)} %get-tuple-element.25), kind=kLoop, calls=%fused_computation.30 | loop fusion | flops 262144 | bytes 1581312 | tf_op jit(solution)/shard_map/neg | solution.py:29
  30.7 7.4 %all-to-all-done = bf16[8,256,256]{2,1,0:T(8,128)(2,1)} async-done(((bf16[8,256,256]{2,1,0:T(8,128)(2,1)}), bf16[8,256,256]{2,1,0:T(8,128)(2,1)}, u32[]{:S(2)}, u32[]{:S(2)}) %all-to-all-start) | async-done | bytes 1048608 | tf_op jit(solution)/shard_map/all_to_all | solution.py:185
  38.0 2.2 fusion.38
  40.3 100.8 %all-gather.2.cloned.1.call-done = bf16[2048,4608]{1,0:T(8,128)(2,1)} async-done(((bf16[128,4608]{1,0:T(8,128)(2,1)}), bf16[2048,4608]{1,0:T(8,128)(2,1)}) %all-gather.2.cloned.1.call-update) | async-done | bytes 18874384 | tf_op jit(solution)/shard_map/all_gather | solution.py:176
  141.1 10.7 %fusion.41 = f32[2048,256]{0,1:T(8,128)} fusion(bf16[2048,4608]{1,0:T(8,128)(2,1)} %all-gather.2.cloned.1.call-done, bf16[4608,256]{1,0:T(8,128)(2,1)} %param.15), kind=kOutput, calls=%fused_computation.116 | convolution fusion | flops 4831838208 | bytes 23330816 | tf_op jit(solution)/shard_map/dot_general | solution.py:194
  151.8 2.9 copy.63
  154.7 3.2 fusion.37
  157.8 3.9 copy.75
  161.8 3.9 copy.76
  165.7 9.3 %fusion.42 = f32[2048,128]{1,0:T(8,128)S(1)} fusion(bf16[2048,4608]{1,0:T(8,128)(2,1)} %all-gather.2.cloned.1.call-done, bf16[4608,128]{1,0:T(8,128)(2,1)} %param.16), kind=kOutput, calls=%fused_computation.117 | convolution fusion | flops 2415919104 | bytes 21102592 | tf_op jit(solution)/shard_map/dot_general | solution.py:195
  175.1 0.3 fusion.39
  175.4 0.9 copy-done.8
  176.3 0.3 copy-done.9
  176.6 0.3 copy-done.10
  176.9 0.9 fusion.9
  177.8 0.7 copy-done.6
  178.5 0.6 copy-done.7
  179.1 2.5 maximum_multiply_fusion
  181.6 0.8 mul.254
  182.4 0.8 copy-done.5
  183.2 0.8 fusion.6.q_ref
  184.0 0.5 copy-done.17
  184.5 9.2 %convolution_convert_fusion.1.v_ref = bf16[2048,128]{1,0:T(8,128)(2,1)S(1)} fusion(bf16[2048,4608]{1,0:T(8,128)(2,1)} %all-gather.2.cloned.1.call-done, bf16[4608,128]{1,0:T(8,128)(2,1)S(1)} %copy-done.17), kind=kOutput, calls=%fused_computation.6 | convolution fusion | flops 2416181248 | bytes 20578304 | tf_op jit(solution)/shard_map/dot_general | solution.py:196
  193.7 33.5 %attention.1 = bf16[2048,256]{1,0:T(8,128)(2,1)S(1)} custom-call(s32[8,16]{1,0:T(8,128)S(1)} %and_convert_fusion.active, bf16[2048,256]{1,0:T(8,128)(2,1)S(1)} %fusion.6.q_ref, bf16[2048,128]{1,0:T(8,128)(2,1)S(1)} %get-tuple-element.16.k_ref, bf16[2048,128]{1,0:T(8,128)(2,1)S(1)} %convolution_convert_fusion.1.v_ref, bf16[2048,128]{1,0:T(8,128)(2,1)S(1)} %copy-done.3, ...), custom_call_target="tpu_custom_call" | custom-call | tf_op jit(solution)/shard_map/attention/pallas_call | solution.py:147
  227.3 9.1 %convolution_convert_fusion = bf16[2048,4608]{1,0:T(8,128)(2,1)} fusion(bf16[2048,256]{1,0:T(8,128)(2,1)S(1)} %attention.1, bf16[256,4608]{1,0:T(8,128)(2,1)S(1)} %copy-done), kind=kOutput, calls=%fused_computation | convolution fusion | flops 4841275392 | bytes 22282240 | tf_op jit(solution)/shard_map/dot_general | solution.py:204
  236.4 0.0 reduce-scatter.2.cloned.1.call-update
  236.4 153.6 %reduce-scatter.2.cloned.1.call-done = bf16[128,4608]{1,0:T(8,128)(2,1)} async-done(((bf16[2048,4608]{1,0:T(8,128)(2,1)}), bf16[128,4608]{1,0:T(8,128)(2,1)}) %reduce-scatter.2.cloned.1.call-update) | async-done | bytes 1179664 | tf_op jit(solution)/shard_map/reduce_scatter | solution.py:203
  390.0 1.6 fusion
  391.6 2.8 fusion.7
  (45 shorter events, 0.2 us)
Async XLA Ops:
  6.5 220.7 %copy-start = (bf16[256,4608]{1,0:T(8,128)(2,1)S(1)}, bf16[256,4608]{1,0:T(8,128)(2,1)}, u32[]{:S(2)}) copy-start(bf16[256,4608]{1,0:T(8,128)(2,1)} %param.18) | copy-start | bytes 7077892
  6.5 4.5 %copy-start.11 = (bf16[8,256,128]{2,1,0:T(8,128)(2,1)S(1)}, bf16[8,256,128]{2,1,0:T(8,128)(2,1)}, u32[]{:S(2)}) copy-start(bf16[8,256,128]{2,1,0:T(8,128)(2,1)} %param.20) | copy-start | bytes 1572868
  6.5 134.6 %all-gather.2.cloned.1.call-start = ((), (), s32[]{:S(2)}) async-start(), calls=%async_computation.2 | async-start | bytes 20054016 | tf_op jit(solution)/shard_map/all_gather | solution.py:176
  8.3 3.1 copy-start.12
  11.0 0.8 copy-start.15
  12.4 8.1 %copy-start.16 = (s32[1,3]{1,0:T(1,128)S(1)}, s32[1,3]{1,0:T(1,128)}, u32[]{:S(2)}) copy-start(s32[1,3]{1,0:T(1,128)} %param.25) | copy-start | bytes 40
  12.4 8.5 %copy-start.14 = (s32[1,8]{1,0:T(1,128)S(1)}, s32[1,8]{1,0:T(1,128)}, u32[]{:S(2)}) copy-start(s32[1,8]{1,0:T(1,128)} %param.23) | copy-start | bytes 100
  12.4 8.9 %copy-start.13 = (s32[1,204]{1,0:T(1,128)S(1)}, s32[1,204]{1,0:T(1,128)}, u32[]{:S(2)}) copy-start(s32[1,204]{1,0:T(1,128)} %param.24) | copy-start | bytes 2452
  13.6 24.4 %all-to-all-start = ((bf16[8,256,256]{2,1,0:T(8,128)(2,1)}), bf16[8,256,256]{2,1,0:T(8,128)(2,1)}, u32[]{:S(2)}, u32[]{:S(2)}) async-start(bf16[8,256,256]{2,1,0:T(8,128)(2,1)} %copy.71), calls=%async_computation | async-start | bytes 2097152 | tf_op jit(solution)/shard_map/all_to_all | solution.py:185
  20.5 369.6 %reduce-scatter.2.cloned.1.call-start = ((), (), s32[]{:S(2)}) async-start(), calls=%async_computation.3 | async-start | bytes 20054016 | tf_op jit(solution)/shard_map/reduce_scatter | solution.py:203
  175.0 1.2 copy-start.8
  175.0 1.5 copy-start.9
  175.0 1.8 copy-start.10
  176.9 1.6 copy-start.6
  176.9 2.2 copy-start.7
  181.6 1.6 copy-start.5
  183.2 1.3 copy-start.17
  184.5 9.2 %copy-start.1 = (s32[2048,1]{1,0:T(8,128)S(1)}, s32[2048,1]{1,0:T(8,128)}, u32[]{:S(2)}) copy-start(s32[2048,1]{1,0:T(8,128)} %copy.72.rcode_ref) | copy-start | bytes 24580
  184.5 9.2 %copy-start.2 = (bf16[2048,128]{1,0:T(8,128)(2,1)S(1)}, bf16[2048,128]{1,0:T(8,128)(2,1)}, u32[]{:S(2)}) copy-start(bf16[2048,128]{1,0:T(8,128)(2,1)} %get-tuple-element.20.pv_ref) | copy-start | bytes 1572868
  184.5 9.2 %copy-start.3 = (bf16[2048,128]{1,0:T(8,128)(2,1)S(1)}, bf16[2048,128]{1,0:T(8,128)(2,1)}, u32[]{:S(2)}) copy-start(bf16[2048,128]{1,0:T(8,128)(2,1)} %get-tuple-element.21.pk_ref) | copy-start | bytes 1572868
  236.4 155.3 %copy-start.4 = (bf16[1,128,4608]{2,1,0:T(8,128)(2,1)S(1)}, bf16[1,128,4608]{2,1,0:T(8,128)(2,1)}, u32[]{:S(2)}) copy-start(bf16[1,128,4608]{2,1,0:T(8,128)(2,1)} %param.13) | copy-start | bytes 3538948
Sparse Core Ops, SparseCore 0:
  11.1 129.9 all-gather.1
  236.5 153.4 reduce-scatter.1

commit v2 on v1

--- a/solution.py
+++ b/solution.py
@@ -163,6 +163,162 @@
     )
 
 
+MESH = pl.DeviceIdType.MESH
+RINGS = 4
+AROUND = 4
+
+
+def place():
+    tok = lax.axis_index("tok")
+    return lax.axis_index("grp"), tok // 8, (tok // 2) % AROUND, tok % 2
+
+
+def device(group, half, spot, core):
+    return (group, half * 8 + lax.rem(spot + 2 * AROUND, AROUND) * 2 + core)
+
+
+def greet(partners):
+    barrier = pltpu.get_barrier_semaphore()
+    for partner in partners:
+        pl.semaphore_signal(barrier, inc=1, device_id=partner, device_id_type=MESH)
+    pl.semaphore_wait(barrier, len(partners))
+
+
+def project_kernel(
+    attn_ref, w0_ref, w1_ref, hid_ref, gain_ref, out_ref,
+    other, product, own, pair_out, pair_in, ring_out, ring_in, result,
+    other_send, other_recv, pair_send, pair_recv, ring_send, ring_recv,
+):
+    group, half, spot, core = place()
+    rows = hid_ref.shape[0]
+    width = hid_ref.shape[1] // RINGS
+    chunk = 2 * rows
+    across = device(group, 1 - half, spot, core)
+    sibling = device(group, half, spot, 1 - core)
+    greet([across, sibling, device(group, half, spot + 1, core), device(group, half, spot - 1, core)])
+
+    def other_copy(j):
+        owner = lax.rem(spot + (3, 1, 2, 0)[j], AROUND)
+        start = pl.multiple_of(((1 - half) * AROUND + owner) * chunk, chunk)
+        return pltpu.make_async_remote_copy(
+            src_ref=attn_ref.at[pl.ds(start, chunk)], dst_ref=other.at[j],
+            send_sem=other_send.at[j], recv_sem=other_recv.at[j],
+            device_id=across, device_id_type=MESH,
+        )
+
+    def pair_copy(s, r):
+        return pltpu.make_async_remote_copy(
+            src_ref=pair_out.at[s, r], dst_ref=pair_in.at[s, r],
+            send_sem=pair_send.at[s, r], recv_sem=pair_recv.at[s, r],
+            device_id=sibling, device_id_type=MESH,
+        )
+
+    def ring_copy(s, r):
+        return pltpu.make_async_remote_copy(
+            src_ref=ring_out.at[s, r], dst_ref=ring_in.at[s, r],
+            send_sem=ring_send.at[s, r], recv_sem=ring_recv.at[s, r],
+            device_id=device(group, half, spot + 1 - 2 * (r // 2), core), device_id_type=MESH,
+        )
+
+    for j in range(4):
+        other_copy(j).start()
+
+    def partial(s, r):
+        owner = lax.rem(spot + (2 * (r // 2) - 1) * (1 + s) + 2 * AROUND, AROUND)
+        slot = (r // 2, 2, 1 - r // 2, 3)[s]
+        start = pl.multiple_of((half * AROUND + owner) * chunk, chunk)
+        columns = pl.ds(pl.multiple_of(r * width, width), width)
+        product[...] = jnp.dot(
+            attn_ref[pl.ds(start, chunk), :], w0_ref[:, columns], preferred_element_type=jnp.float32
+        ) + jnp.dot(other[slot], w1_ref[:, columns], preferred_element_type=jnp.float32)
+        theirs = pl.ds(pl.multiple_of((1 - core) * rows, rows), rows)
+        pair_out[s, r] = product[theirs, :].astype(jnp.bfloat16)
+        pair_copy(s, r).start()
+        own[s, r] = product[pl.ds(pl.multiple_of(core * rows, rows), rows), :]
+
+    def partials(s, first, last):
+        def step(r, carry):
+            partial(s, r)
+            return carry
+
+        lax.fori_loop(first, last, step, 0)
+
+    def forward(s):
+        def step(r, carry):
+            pair_copy(s, r).wait_recv()
+            running = own[s, r] + pair_in[s, r].astype(jnp.float32)
+            if s > 0:
+                ring_copy(s - 1, r).wait_recv()
+                running = running + ring_in[s - 1, r].astype(jnp.float32)
+            if s < 3:
+                ring_out[s, r] = running.astype(jnp.bfloat16)
+                ring_copy(s, r).start()
+            else:
+                result[:, pl.ds(pl.multiple_of(r * width, width), width)] = running
+            return carry
+
+        for r in (0, 2, 1, 3):
+            step(r, 0)
+
+    other_copy(0).wait_recv()
+    partials(0, 0, 2)
+    other_copy(1).wait_recv()
+    partials(0, 2, 4)
+    forward(0)
+    other_copy(2).wait_recv()
+    partials(1, 0, 4)
+    partials(2, 0, 4)
+    other_copy(3).wait_recv()
+    partials(3, 0, 4)
+    forward(1)
+    forward(2)
+    forward(3)
+    for j in range(4):
+        other_copy(j).wait_send()
+
+    def drain(r, carry):
+        for s in range(4):
+            pair_copy(s, r).wait_send()
+        for s in range(3):
+            ring_copy(s, r).wait_send()
+        return carry
+
+    lax.fori_loop(0, RINGS, drain, 0)
+    projected = result[...]
+    scale = lax.rsqrt(jnp.mean(projected * projected, axis=-1, keepdims=True) + EPSILON)
+    out_ref[...] = (
+        hid_ref[...].astype(jnp.float32) + projected * scale * gain_ref[...]
+    ).astype(jnp.bfloat16)
+
+
+def project(attended, w_own, w_across, own_rows, post_gain):
+    rows, features = own_rows.shape
+    width = features // RINGS
+    vmem = pl.BlockSpec(memory_space=pltpu.VMEM)
+    dma = pltpu.SemaphoreType.DMA
+    return pl.pallas_call(
+        project_kernel,
+        out_shape=jax.ShapeDtypeStruct((rows, features), jnp.bfloat16),
+        in_specs=[vmem] * 5,
+        out_specs=vmem,
+        scratch_shapes=[
+            pltpu.VMEM((4, 2 * rows, attended.shape[1]), jnp.bfloat16),
+            pltpu.VMEM((2 * rows, width), jnp.float32),
+            pltpu.VMEM((4, RINGS, rows, width), jnp.float32),
+            pltpu.VMEM((4, RINGS, rows, width), jnp.bfloat16),
+            pltpu.VMEM((4, RINGS, rows, width), jnp.bfloat16),
+            pltpu.VMEM((3, RINGS, rows, width), jnp.bfloat16),
+            pltpu.VMEM((3, RINGS, rows, width), jnp.bfloat16),
+            pltpu.VMEM((rows, features), jnp.float32),
+            dma((4,)), dma((4,)), dma((4, RINGS)), dma((4, RINGS)), dma((3, RINGS)), dma((3, RINGS)),
+        ],
+        compiler_params=pltpu.CompilerParams(
+            collective_id=1, has_side_effects=True, vmem_limit_bytes=56 << 20
+        ),
+        name="project",
+    )(attended, w_own, w_across, own_rows, post_gain[None, :])
+
+
 def on_device(
     hidden, input_gain, w_query, w_key, w_value, w_out, post_gain, cache_keys, cache_values,
     page_table, stretch_request, recompute_ids, query_counts,
@@ -173,6 +329,12 @@
     new_rows = own_rows.shape[0] * tok_total
     pages, stretch_len = cache_keys.shape[:2]
     normed_own = normalize(own_rows, input_gain).astype(jnp.bfloat16)
+    there = [
+        ((g + groups // 2) % groups) * tok_total + (t + tok_total // 2) % tok_total
+        for g in range(groups)
+        for t in range(tok_total)
+    ]
+    w_across = lax.ppermute(w_out, ("grp", "tok"), list(enumerate(there)))
     segment = lax.all_gather(normed_own, "tok", axis=0, tiled=True)
     group = lax.axis_index("grp")
     mine = page_table // pages == group
@@ -200,14 +362,8 @@
     attended = attention(
         q, k, v.astype(jnp.bfloat16), got[:, :HEAD], got[:, HEAD:], pcos, psin, row_code, key_code, live
     )
-    summed = lax.psum_scatter(
-        jnp.dot(attended, w_out, preferred_element_type=jnp.float32).astype(jnp.bfloat16),
-        "tok",
-        scatter_dimension=0,
-        tiled=True,
-    ).astype(jnp.float32)
-    result = own_rows.astype(jnp.float32) + normalize(summed, post_gain)
-    return result.astype(jnp.bfloat16)[None]
+    output = project(attended, w_out, w_across, own_rows, post_gain)
+    return output[None]
 
 
 def solution(mesh):

time: 402 us -> 289 us (0.72)
  waiting for transfers between devices: 262 us -> 105 us
  Pallas kernels: 33.5 us -> 85.6 us
  matrix products: 38.8 us -> 28 us
    reduce_scatter x1 -> x0, waiting for transfers between devices: 154 us -> none  [on_device(): lax.psum_scatter(jnp.dot(attended, w_out, preferred_element_type=jnp.floa...]
    pallas_call x0 -> x1, Pallas kernels: none -> 57 us  [project(): pl.pallas_call(project_kernel, out_shape=jax.ShapeDtypeStruct((rows, feat...]
    dot_general x1 -> x0, matrix products: 9.09 us -> none  [on_device(): jnp.dot(attended, w_out, preferred_element_type=jnp.float32)]
    pallas_call x1, Pallas kernels: 33.5 us -> 28.5 us  [attention(): pl.pallas_call(attention_kernel, out_shape=jax.ShapeDtypeStruct((rows, q....]
    unnamed x42 -> x47, local copies, waits for them, and re-layouts: 12.7 us -> 15.6 us
  transfers between devices with their start and end apart: 3 -> 3, of which waited for: 3 -> 2; matrix products, arithmetic and copies ran while one was open for 4% -> 22% of each run, Pallas kernels for 0% -> 10%
where the time goes in v2:
time: 289 us; the launch traced here: 288 us
  waiting for transfers between devices  105 us (36%)
  Pallas kernels  85.6 us (30%)
  matrix products  28 us (10%)
  local copies, waits for them, and re-layouts  26.2 us (9%)
  other arithmetic  19.8 us (7%)
  between operations  13.8 us (5%)
  starting transfers between devices  9.78 us (3%)
    all_gather x1, waiting for transfers between devices, on_device(): segment = lax.all_gather(normed_own, 'tok', axis=0, tiled=True)  101 us
    pallas_call x1, Pallas kernels, project(): pl.pallas_call(project_kernel, out_shape=jax.ShapeDtypeStruct((rows, feat...  57 us
    pallas_call x1, Pallas kernels, attention(): pl.pallas_call(attention_kernel, out_shape=jax.ShapeDtypeStruct((rows, q....  28.5 us
    unnamed x47, local copies, waits for them, and re-layouts  15.6 us
    dot_general x1, matrix products, on_device(): k = jnp.dot(segment, w_key, preferred_element_type=jnp.float32)  9.31 us
    dot_general x1, matrix products, on_device(): v = jnp.dot(segment, w_value, preferred_element_type=jnp.float32)  9.23 us
    dot_general x1, matrix products, on_device(): q = jnp.dot(segment, w_query, preferred_element_type=jnp.float32)  9.02 us
    all_to_all x1, starting transfers between devices, on_device(): got = lax.all_to_all(send, 'grp', 0, 0, tiled=True)  6.88 us
  transfers between devices with their start and end apart: 3, of which 2 were waited for; matrix products, arithmetic and copies ran while one was open for 22% of the time, Pallas kernels for 10%

profile of v2, /device:TPU:1, one launch (start us, length us, event | category | flops | bytes accessed | tf_op | source)
XLA Modules:
  0.0 288.0 jit_solution(2271931281648014146)
XLA Ops:
  6.5 1.7 fusion
  8.3 0.0 copy-start.13
  8.3 2.7 fusion.2
  11.0 0.0 all-gather.2.cloned.1.call-update
  11.0 0.3 copy.69
  11.4 0.3 copy.70
  11.8 0.1 fusion.18
  11.9 0.5 convolution_convert_fusion.1
  12.4 0.0 copy-start.18
  12.4 0.0 copy-start.16
  12.4 0.0 copy-start.15
  12.4 0.0 copy-start.14
  12.4 1.2 copy.71
  13.6 6.9 %all-to-all-start = ((bf16[8,256,256]{2,1,0:T(8,128)(2,1)}), bf16[8,256,256]{2,1,0:T(8,128)(2,1)}, u32[]{:S(2)}, u32[]{:S(2)}) async-start(bf16[8,256,256]{2,1,0:T(8,128)(2,1)} %copy.71), calls=%async_computation | async-start | bytes 2097152 | tf_op jit(solution)/shard_map/all_to_all | solution.py:347
  20.5 2.9 %collective-permute-start = (bf16[256,4608]{1,0:T(8,128)(2,1)}, bf16[256,4608]{1,0:T(8,128)(2,1)}, u32[]{:S(2)}, u32[]{:S(2)}) collective-permute-start(bf16[256,4608]{1,0:T(8,128)(2,1)} %w0_ref.1), channel_id=1, source_target_pairs={{0,72},{1,73},{2,74},{3,75},{4,76},{5,77},{6,78},{7,79},{8,64},{9,... | collective-permute-start | bytes 7077896 | tf_op jit(solution)/shard_map/ppermute | solution.py:337
  23.4 0.2 reduce-window.4
  23.6 0.1 slice.23
  23.7 0.1 fusion.10
  23.8 0.1 convert_reduce_fusion.1
  23.9 0.1 select_reduce_fusion.6
  24.1 0.1 select_reduce_fusion
  24.2 0.1 select_reduce_fusion.1
  24.3 0.1 fusion.15
  24.4 0.1 select_reduce_fusion.3
  24.6 0.1 add_bitcast_fusion
  24.7 0.1 fusion.26
  24.8 0.1 pad_maximum_fusion.2.pcos_ref
  24.9 0.2 fusion.32
  25.0 0.3 compare_reduce_fusion
  25.4 0.1 fusion.14
  25.5 0.1 fusion.23
  25.5 0.1 pad_maximum_fusion.3.psin_ref
  25.6 0.6 broadcast_in_dim.16.gain_ref
  26.2 0.4 copy.73.live_ref
  26.6 1.4 copy.72.rcode_ref
  28.0 0.1 fusion.12
  28.2 0.1 and_convert_fusion.active
  28.2 5.9 %fusion.9 = (f32[2048,64]{1,0:T(8,128)}, f32[2048,64]{1,0:T(8,128)}, f32[2048,64]{1,0:T(8,128)}) fusion(f32[64]{0:T(128)S(1)} %multiply_exponential_fusion, f32[2048]{0:T(1024)S(1)} %get-tuple-element.25), kind=kLoop, calls=%fused_computation.22 | loop fusion | flops 262144 | bytes 1581312 | tf_op jit(solution)/shard_map/neg | solution.py:29
  34.2 4.0 %all-to-all-done = bf16[8,256,256]{2,1,0:T(8,128)(2,1)} async-done(((bf16[8,256,256]{2,1,0:T(8,128)(2,1)}), bf16[8,256,256]{2,1,0:T(8,128)(2,1)}, u32[]{:S(2)}, u32[]{:S(2)}) %all-to-all-start) | async-done | bytes 1048608 | tf_op jit(solution)/shard_map/all_to_all | solution.py:347
  38.2 2.3 fusion.34
  40.5 100.7 %all-gather.2.cloned.1.call-done = bf16[2048,4608]{1,0:T(8,128)(2,1)} async-done(((bf16[128,4608]{1,0:T(8,128)(2,1)}), bf16[2048,4608]{1,0:T(8,128)(2,1)}) %all-gather.2.cloned.1.call-update) | async-done | bytes 18874384 | tf_op jit(solution)/shard_map/all_gather | solution.py:338
  141.2 9.3 %fusion.38 = f32[2048,128]{1,0:T(8,128)S(1)} fusion(bf16[2048,4608]{1,0:T(8,128)(2,1)} %all-gather.2.cloned.1.call-done, bf16[4608,128]{1,0:T(8,128)(2,1)} %param.16), kind=kOutput, calls=%fused_computation.108 | convolution fusion | flops 2415919104 | bytes 21102592 | tf_op jit(solution)/shard_map/dot_general | solution.py:357
  150.5 0.3 fusion.35
  150.9 0.9 copy-done.9
  151.7 0.3 copy-done.10
  152.0 0.3 copy-done.11
  152.4 2.5 fusion.5
  154.8 9.0 %fusion.37 = f32[2048,256]{0,1:T(8,128)S(1)} fusion(bf16[2048,4608]{1,0:T(8,128)(2,1)} %all-gather.2.cloned.1.call-done, bf16[4608,256]{1,0:T(8,128)(2,1)S(1)} %copy-done), kind=kOutput, calls=%fused_computation.107 | convolution fusion | flops 4831838208 | bytes 23330816 | tf_op jit(solution)/shard_map/dot_general | solution.py:356
  163.9 1.3 copy-done.7
  165.2 1.6 fusion.33
  166.8 1.9 copy.63
  168.7 4.0 %copy.75 = f32[2048,2,64]{2,1,0:T(2,128)} copy(f32[2048,2,64]{0,2,1:T(8,128)} %get-tuple-element.18) | data formatting | bytes 2097152
  172.7 3.9 %copy.76 = f32[2048,2,64]{2,1,0:T(2,128)} copy(f32[2048,2,64]{0,2,1:T(8,128)} %get-tuple-element.19) | data formatting | bytes 2097152
  176.6 4.3 %maximum_multiply_fusion = f32[2048,2,128]{2,1,0:T(2,128)S(1)} fusion(f32[2048,2,64]{2,1,0:T(2,128)} %copy.76, f32[2048,2,64]{2,1,0:T(2,128)} %copy.75, f32[2048,128]{1,0:T(8,128)} %get-tuple-element.17), kind=kLoop, calls=%fused_computation.9 | loop fusion | flops 1048576 | bytes 5242880 | tf_op jit(solution)/shard_map/mul | solution.py:36
  180.9 0.8 mul.235
  181.7 0.0 copy-start.19
  181.7 0.5 fusion.3.q_ref
  182.2 0.8 copy-done.19
  183.0 9.2 %convolution_convert_fusion.v_ref = bf16[2048,128]{1,0:T(8,128)(2,1)S(1)} fusion(bf16[2048,4608]{1,0:T(8,128)(2,1)} %all-gather.2.cloned.1.call-done, bf16[4608,128]{1,0:T(8,128)(2,1)S(1)} %copy-done.19), kind=kOutput, calls=%fused_computation.2 | convolution fusion | flops 2416181248 | bytes 20578304 | tf_op jit(solution)/shard_map/dot_general | solution.py:358
  192.2 28.5 %attention.1.attn_ref = bf16[2048,256]{1,0:T(8,128)(2,1)S(1)} custom-call(s32[8,16]{1,0:T(8,128)S(1)} %and_convert_fusion.active, bf16[2048,256]{1,0:T(8,128)(2,1)S(1)} %fusion.3.q_ref, bf16[2048,128]{1,0:T(8,128)(2,1)S(1)} %copy-done.4, bf16[2048,128]{1,0:T(8,128)(2,1)S(1)} %convolution_convert_fusion.v_ref, bf16[2048,128]{1,0:T(8,128)(2,1)S(1)} %copy-done.6, ...), custom_call_target="tpu_custom_call" | custom-call | tf_op jit(solution)/shard_map/attention/pallas_call | solution.py:147
  220.8 0.0 copy-start.2
  220.8 1.0 copy-done.2
  221.8 57.0 %project.1 = bf16[128,4608]{1,0:T(8,128)(2,1)} custom-call(bf16[2048,256]{1,0:T(8,128)(2,1)} %copy-done.2, bf16[256,4608]{1,0:T(8,128)(2,1)} %w0_ref.1, bf16[256,4608]{1,0:T(8,128)(2,1)} %collective-permute-done.w1_ref, bf16[128,4608]{1,0:T(8,128)(2,1)} %bitcast.55, f32[1,4608]{1,0:T(1,128)} %broadcast_in_dim.16.gain_ref), custom_call_target="tpu_custom_call" | custom-call | tf_op jit(solution)/shard_map/project/pallas_call | solution.py:299
  278.8 2.4 copy.84
  (47 shorter events, 0.2 us)
Async XLA Ops:
  6.5 148.3 %copy-start = (bf16[4608,256]{1,0:T(8,128)(2,1)S(1)}, bf16[4608,256]{1,0:T(8,128)(2,1)}, u32[]{:S(2)}) copy-start(bf16[4608,256]{1,0:T(8,128)(2,1)} %param.15) | copy-start | bytes 7077892
  6.5 4.5 %copy-start.12 = (bf16[8,256,128]{2,1,0:T(8,128)(2,1)S(1)}, bf16[8,256,128]{2,1,0:T(8,128)(2,1)}, u32[]{:S(2)}) copy-start(bf16[8,256,128]{2,1,0:T(8,128)(2,1)} %param.20) | copy-start | bytes 1572868
  6.5 134.6 %all-gather.2.cloned.1.call-start = ((), (), s32[]{:S(2)}) async-start(), calls=%async_computation.1 | async-start | bytes 20054016 | tf_op jit(solution)/shard_map/all_gather | solution.py:338
  8.3 3.1 %copy-start.13 = (bf16[8,256,128]{2,1,0:T(8,128)(2,1)S(1)}, bf16[8,256,128]{2,1,0:T(8,128)(2,1)}, u32[]{:S(2)}) copy-start(bf16[8,256,128]{2,1,0:T(8,128)(2,1)} %param.21) | copy-start | bytes 1572868
  11.0 0.8 copy-start.17
  12.4 11.0 %copy-start.18 = (s32[1,3]{1,0:T(1,128)S(1)}, s32[1,3]{1,0:T(1,128)}, u32[]{:S(2)}) copy-start(s32[1,3]{1,0:T(1,128)} %param.25) | copy-start | bytes 40
  12.4 11.4 %copy-start.16 = (s32[1,8]{1,0:T(1,128)S(1)}, s32[1,8]{1,0:T(1,128)}, u32[]{:S(2)}) copy-start(s32[1,8]{1,0:T(1,128)} %param.23) | copy-start | bytes 100
  12.4 11.8 %copy-start.15 = (s32[1,204]{1,0:T(1,128)S(1)}, s32[1,204]{1,0:T(1,128)}, u32[]{:S(2)}) copy-start(s32[1,204]{1,0:T(1,128)} %param.24) | copy-start | bytes 2452
  12.4 13.2 %copy-start.14 = (f32[4608]{0:T(1024)S(1)}, f32[4608]{0:T(1024)}, u32[]{:S(2)}) copy-start(f32[4608]{0:T(1024)} %param.19) | copy-start | bytes 55300
  13.6 24.5 %all-to-all-start = ((bf16[8,256,256]{2,1,0:T(8,128)(2,1)}), bf16[8,256,256]{2,1,0:T(8,128)(2,1)}, u32[]{:S(2)}, u32[]{:S(2)}) async-start(bf16[8,256,256]{2,1,0:T(8,128)(2,1)} %copy.71), calls=%async_computation | async-start | bytes 2097152 | tf_op jit(solution)/shard_map/all_to_all | solution.py:347
  20.5 201.2 %collective-permute-start = (bf16[256,4608]{1,0:T(8,128)(2,1)}, bf16[256,4608]{1,0:T(8,128)(2,1)}, u32[]{:S(2)}, u32[]{:S(2)}) collective-permute-start(bf16[256,4608]{1,0:T(8,128)(2,1)} %w0_ref.1), channel_id=1, source_target_pairs={{0,72},{1,73},{2,74},{3,75},{4,76},{5,77},{6,78},{7,79},{8,64},{9,... | collective-permute-start | bytes 7077896 | tf_op jit(solution)/shard_map/ppermute | solution.py:337
  150.5 1.2 copy-start.9
  150.5 1.5 copy-start.10
  150.5 1.8 copy-start.11
  163.9 1.3 copy-start.7
  176.6 4.3 %copy-start.8 = (f32[2048,128]{1,0:T(8,128)S(1)}, f32[2048,128]{1,0:T(8,128)}, u32[]{:S(2)}) copy-start(f32[2048,128]{1,0:T(8,128)} %get-tuple-element.22) | copy-start | bytes 3145732
  181.7 1.3 copy-start.19
  182.9 9.2 %copy-start.3 = (s32[2048,1]{1,0:T(8,128)S(1)}, s32[2048,1]{1,0:T(8,128)}, u32[]{:S(2)}) copy-start(s32[2048,1]{1,0:T(8,128)} %copy.72.rcode_ref) | copy-start | bytes 24580
  182.9 9.3 %copy-start.4 = (bf16[2048,128]{1,0:T(8,128)(2,1)S(1)}, bf16[2048,128]{1,0:T(8,128)(2,1)}, u32[]{:S(2)}) copy-start(bf16[2048,128]{1,0:T(8,128)(2,1)} %get-tuple-element.16.k_ref) | copy-start | bytes 1572868
  182.9 9.3 %copy-start.5 = (bf16[2048,128]{1,0:T(8,128)(2,1)S(1)}, bf16[2048,128]{1,0:T(8,128)(2,1)}, u32[]{:S(2)}) copy-start(bf16[2048,128]{1,0:T(8,128)(2,1)} %get-tuple-element.20.pv_ref) | copy-start | bytes 1572868
  182.9 9.3 %copy-start.6 = (bf16[2048,128]{1,0:T(8,128)(2,1)S(1)}, bf16[2048,128]{1,0:T(8,128)(2,1)}, u32[]{:S(2)}) copy-start(bf16[2048,128]{1,0:T(8,128)(2,1)} %get-tuple-element.21.pk_ref) | copy-start | bytes 1572868
  220.8 1.0 copy-start.2
  221.8 59.4 %copy-start.1 = (bf16[4608,256]{1,0:T(8,128)(2,1)S(1)}, bf16[4608,256]{1,0:T(8,128)(2,1)}, u32[]{:S(2)}) copy-start(bf16[4608,256]{1,0:T(8,128)(2,1)} %param.15) | copy-start | bytes 7077892
Sparse Core Ops, SparseCore 0:
  11.1 129.9 all-gather.1
